TPU v7x, 256 devices: a whole 4x4x8 slice. The times are simulated.
256 devices in a mesh: bubble: 16 (over y_hi, z), panel: 16 (over y_lo, x, core).
Axes of the slice: x: 4, y: 4 (y_hi: 2, y_lo: 2; y = y_hi * 2 + y_lo), z: 8, core: 2. Of those that a mesh axis runs over, the one named last changes fastest.
Arguments:
- density: float32 [128, 12288], P('bubble', 'panel'), may hold values from -6 to 6
- right_side: float32 [128, 12288], P('bubble', 'panel'), may hold values from -6 to 6
- inv_diag: bfloat16 [128, 96, 128, 128], P('bubble', 'panel')
- near_vals: bfloat16 [128, 96, 4, 128, 128], P('bubble', 'panel'), may hold values from -0.25 to 0.25
- near_bubble: int32 [128, 96, 4], P('bubble', 'panel'), may hold values from 0 to 127, as said below
- near_block: int32 [128, 96, 4], P('bubble', 'panel'), may hold values from 0 to 95
- near_count: int32 [128, 96], P('bubble', 'panel'), may hold values from 1 to 4, as said below
- colour: int32 [128], P('bubble'), may hold values from 0 to 1
- moment_map: bfloat16 [128, 16, 12288], P('bubble', None, 'panel'), may hold values from -0.0546875 to 0.0546875
- spread_map: bfloat16 [128, 16, 12288], P('bubble', None, 'panel'), may hold values from -0.125 to 0.125
- centres: float32 [3, 128], replicated, may hold values from 0.2 to 6
Outputs:
- relaxed: float32 [128, 12288], P('bubble', 'panel')
Inputs may be any that keep to these rules, and one draw needn't show every extreme that they name: `near_bubble`: every slot of bubble b names a bubble within 8 of b. `near_count`: the first row block of every bubble uses all 4 slots.
All inputs are finite; a program needn't handle non-finite values.
Results may differ from a plain program's by a relative error of at most 0.0041.
Values may be sent and summed in bfloat16 or wider, within the bound.
No kernel may reach another device: no remote copies, remote signals or barrier semaphores. Data moves between devices by JAX's collectives and lax.ppermute only.
A program may use at most 64 MiB of HBM per device.

v0:
```python
import jax
import jax.numpy as jnp
from jax import lax
from jax.sharding import PartitionSpec as P


def with_halo(shard, sides, width):
    for axis, dim in sides:
        peers, length = (lax.axis_size(axis), shard.shape[dim])
        up = [(i, (i + 1) % peers) for i in range(peers - 1)]
        down = [(j, i) for i, j in up]
        last = lax.slice_in_dim(shard, length - width, length, axis=dim)
        first = lax.slice_in_dim(shard, 0, width, axis=dim)
        before = lax.ppermute(last, axis, up)
        after = lax.ppermute(first, axis, down)
        shard = jnp.concatenate([before, shard, after], axis=dim)
    return shard


def near_field(
    neighbourhood, near_vals, near_bubble, near_block, near_count, first_bubble, block_size
):
    rim_count = neighbourhood.shape[0]
    blocks = neighbourhood.reshape(rim_count, neighbourhood.shape[1] // block_size, block_size)
    local_bubble = near_bubble - first_bubble
    sources = blocks[local_bubble, near_block]
    live_slot = jnp.arange(near_vals.shape[2])[None, None, :] < near_count[:, :, None]
    sources = jnp.where(live_slot[:, :, :, None], sources, jnp.zeros_like(sources))
    return jnp.einsum("brsij,brsj->bri", near_vals, sources, preferred_element_type=jnp.float32)


def far_kernel(centres, my_bubbles, reach):
    centre_mine = centres[:, my_bubbles]
    diff = centre_mine[:, :, None] - centres[:, None, :]
    direct_sq = jnp.sum(diff * diff, axis=0)
    mirrored = centre_mine[2][:, None] + centres[2][None, :]
    image_sq = diff[0] * diff[0] + diff[1] * diff[1] + mirrored * mirrored
    kernel = 1.0 / jnp.sqrt(direct_sq + 1.0) + 1.0 / jnp.sqrt(image_sq + 1.0)
    gap = jnp.abs(my_bubbles[:, None] - jnp.arange(centres.shape[1])[None, :])
    return jnp.where(gap > reach, kernel, jnp.zeros_like(kernel))


def per_device(
    density,
    right_side,
    inv_diag,
    near_vals,
    near_bubble,
    near_block,
    near_count,
    colour,
    moment_map,
    spread_map,
    centres,
):
    bub_dev = density.shape[0]
    panels_dev = density.shape[1]
    block_size = inv_diag.shape[2]
    my_index = lax.axis_index("bubble")
    my_bubbles = my_index * bub_dev + jnp.arange(bub_dev, dtype=jnp.int32)
    first_bubble = my_index * bub_dev - bub_dev
    kernel = far_kernel(centres, my_bubbles, bub_dev)
    relaxed = density
    for colour_now in range(2):
        dens_bf = relaxed.astype(jnp.bfloat16)
        panel_full = lax.all_gather(dens_bf, "panel", axis=1, tiled=True)
        neighbourhood = with_halo(panel_full, (("bubble", 0),), bub_dev)
        near = near_field(
            neighbourhood, near_vals, near_bubble, near_block, near_count, first_bubble, block_size
        )
        partial_value = jnp.einsum(
            "bki,bi->bk", moment_map, dens_bf, preferred_element_type=jnp.float32
        )
        own_moments = lax.psum(partial_value, "panel")
        all_moments = lax.all_gather(own_moments, "bubble", axis=0, tiled=True)
        far_coeff = jnp.dot(kernel, all_moments, precision=lax.Precision.HIGHEST).astype(
            jnp.bfloat16
        )
        far = jnp.einsum("bki,bk->bi", spread_map, far_coeff, preferred_element_type=jnp.float32)
        remainder = (right_side - near.reshape(bub_dev, panels_dev) - far).astype(jnp.bfloat16)
        remainder = remainder.reshape(bub_dev, panels_dev // block_size, block_size)
        updated = jnp.einsum(
            "brij,brj->bri", inv_diag, remainder, preferred_element_type=jnp.float32
        )
        relaxed = jnp.where(
            (colour == colour_now)[:, None], updated.reshape(bub_dev, panels_dev), relaxed
        )
    return relaxed


def solution(mesh):
    in_specs = (
        P("bubble", "panel"),
        P("bubble", "panel"),
        P("bubble", "panel", None, None),
        P("bubble", "panel", None, None, None),
        P("bubble", "panel", None),
        P("bubble", "panel", None),
        P("bubble", "panel"),
        P("bubble"),
        P("bubble", None, "panel"),
        P("bubble", None, "panel"),
        P(),
    )
    out_specs = P("bubble", "panel")
    return jax.shard_map(
        per_device, mesh=mesh, in_specs=in_specs, out_specs=out_specs, check_vma=False
    )
```

profile of v0, /device:TPU:24, one launch (start us, length us, event | category | flops | bytes accessed | tf_op | source)
XLA Modules:
  0.0 213.0 jit_solution(4248419762880765899)
XLA Ops:
  0.0 0.9 convert_element_type.18
  0.9 19.4 %all_gather.12 = bf16[8,12288]{1,0:T(8,128)(2,1)S(1)} all-gather(bf16[8,768]{1,0:T(8,128)(2,1)S(1)} %convert_element_type.18), channel_id=1, replica_groups=mesh['bubble'=16,'panel'=16] {'panel'}, dimensions={1}, use_global_device_ids=true | all-gather | bytes 208896 | tf_op jit(solution)/shard_map/all_gather | solution.py:66
  20.2 3.8 %collective-permute-start = (bf16[8,12288]{1,0:T(8,128)(2,1)S(1)}, bf16[8,12288]{1,0:T(8,128)(2,1)S(1)}, u32[]{:S(2)}, u32[]{:S(2)}) collective-permute-start(bf16[8,12288]{1,0:T(8,128)(2,1)S(1)} %all_gather.12), channel_id=1, source_target_pairs={{0,16},{16,32},{32,48},{48,64},{64,80},{80,96},{96,112},{112,128},... | collective-permute-start | bytes 589832 | tf_op jit(solution)/shard_map/ppermute | solution.py:14
  24.0 6.2 %collective-permute-start.1 = (bf16[8,12288]{1,0:T(8,128)(2,1)S(1)}, bf16[8,12288]{1,0:T(8,128)(2,1)S(1)}, u32[]{:S(2)}, u32[]{:S(2)}) collective-permute-start(bf16[8,12288]{1,0:T(8,128)(2,1)S(1)} %all_gather.12), channel_id=1, source_target_pairs={{16,0},{32,16},{48,32},{64,48},{80,64},{96,80},{112,96},{128,112},... | collective-permute-start | bytes 589832 | tf_op jit(solution)/shard_map/ppermute | solution.py:15
  30.3 0.8 copy.18
  31.1 0.6 gather_fusion.1
  31.7 0.1 copy.19
  31.8 0.2 slice_reduce_fusion
  31.9 0.7 slice_bitcast_fusion
  32.6 0.7 convert_bitcast_fusion
  33.4 0.8 multiply_reduce_fusion
  34.1 1.1 fusion.16
  35.2 27.2 %psum.14 = f32[8,16]{1,0:T(8,128)S(1)} all-reduce(f32[8,16]{1,0:T(8,128)S(1)} %bitcast.107), channel_id=1, replica_groups=mesh['bubble'=16,'panel'=16] {'panel'}, use_global_device_ids=true, to_apply=%region_1.2 | all-reduce | flops 128 | bytes 1024 | tf_op jit(solution)/shard_map/psum | solution.py:74
  62.4 37.8 %all_gather.13 = f32[128,16]{1,0:T(8,128)S(1)} all-gather(f32[8,16]{1,0:T(8,128)S(1)} %psum.14), channel_id=1, replica_groups=mesh['bubble'=16,'panel'=16] {'bubble'}, dimensions={0}, use_global_device_ids=true | all-gather | bytes 8704 | tf_op jit(solution)/shard_map/all_gather | solution.py:75
  100.2 0.7 fusion.22
  101.0 0.1 copy.17
  101.1 0.1 reshape.62
  101.2 0.8 iota_compare_fusion
  101.9 0.1 fusion.31
  102.0 0.2 fusion
  102.2 1.1 fusion.34
  103.3 0.7 broadcast_compare_fusion.1
  103.9 0.0 collective-permute-done
  103.9 0.0 collective-permute-done.1
  104.0 0.1 copy.36
  104.1 2.5 %gather_fusion = bf16[192,128]{1,0:T(8,128)(2,1)S(1)} fusion(bf16[24,96,128]{2,1,0:T(8,128)(2,1)S(1)} %bitcast.101, s32[192]{0:T(256)S(1)} %reshape.62), kind=kCustom, calls=%fused_computation | custom fusion | bytes 99840 | tf_op jit(solution)/shard_map/gather | solution.py:26
  106.6 0.1 select_bitcast_fusion.1
  106.7 0.0 copy-start.3
  106.8 4.5 %fusion.4 = f32[8,6,1,128,1]{3,2,4,1,0:T(1,128)S(1)} fusion(bf16[8,6,4,128,128]{4,3,2,1,0:T(8,128)(2,1)} %param.14, bf16[8,6,4,128,1]{3,2,1,0,4:T(4,128)(2,1)S(1)} %select_bitcast_fusion.1), kind=kOutput, calls=%fused_computation.11 | convolution fusion | flops 6291456 | bytes 6365184 | tf_op jit(solution)/shard_map/brsij,brsj->bri/dot_general | solution.py:29
  111.3 0.0 copy-start.1
  111.3 0.9 fusion.14
  112.2 0.1 fusion.36
  112.3 16.5 %all_gather.14 = bf16[8,12288]{1,0:T(8,128)(2,1)S(1)} all-gather(bf16[8,768]{1,0:T(8,128)(2,1)S(1)} %fusion.36), channel_id=1, replica_groups=mesh['bubble'=16,'panel'=16] {'panel'}, dimensions={1}, use_global_device_ids=true | all-gather | bytes 208896 | tf_op jit(solution)/shard_map/all_gather | solution.py:66
  128.8 2.0 collective-permute-start.2
  130.8 7.5 %collective-permute-start.3 = (bf16[8,12288]{1,0:T(8,128)(2,1)S(1)}, bf16[8,12288]{1,0:T(8,128)(2,1)S(1)}, u32[]{:S(2)}, u32[]{:S(2)}) collective-permute-start(bf16[8,12288]{1,0:T(8,128)(2,1)S(1)} %all_gather.14), channel_id=1, source_target_pairs={{16,0},{32,16},{48,32},{64,48},{80,64},{96,80},{112,96},{128,112},... | collective-permute-start | bytes 589832 | tf_op jit(solution)/shard_map/ppermute | solution.py:15
  138.3 0.2 fusion.12
  138.4 28.5 %psum.15 = f32[8,16]{1,0:T(8,128)S(1)} all-reduce(f32[8,16]{1,0:T(8,128)S(1)} %bitcast.108), channel_id=1, replica_groups=mesh['bubble'=16,'panel'=16] {'panel'}, use_global_device_ids=true, to_apply=%region_2.3 | all-reduce | flops 128 | bytes 1024 | tf_op jit(solution)/shard_map/psum | solution.py:74
  166.9 36.7 %all_gather.15 = f32[128,16]{1,0:T(8,128)S(1)} all-gather(f32[8,16]{1,0:T(8,128)S(1)} %psum.15), channel_id=1, replica_groups=mesh['bubble'=16,'panel'=16] {'bubble'}, dimensions={0}, use_global_device_ids=true | all-gather | bytes 8704 | tf_op jit(solution)/shard_map/all_gather | solution.py:75
  203.7 0.2 fusion.1
  203.8 0.2 fusion.32
  204.0 0.0 collective-permute-done.2
  204.0 0.0 collective-permute-done.3
  204.1 0.1 copy.37
  204.2 2.5 %gather_fusion.2 = bf16[192,128]{1,0:T(8,128)(2,1)S(1)} fusion(bf16[24,96,128]{2,1,0:T(8,128)(2,1)S(1)} %bitcast.100, s32[192]{0:T(256)S(1)} %reshape.62), kind=kCustom, calls=%fused_computation.2 | custom fusion | bytes 99840 | tf_op jit(solution)/shard_map/gather | solution.py:26
  206.7 0.1 select_bitcast_fusion
  206.8 4.5 %fusion.2 = f32[8,6,1,128,1]{3,2,4,1,0:T(1,128)S(1)} fusion(bf16[8,6,4,128,128]{4,3,2,1,0:T(8,128)(2,1)} %param.14, bf16[8,6,4,128,1]{3,2,1,0,4:T(4,128)(2,1)S(1)} %select_bitcast_fusion), kind=kOutput, calls=%fused_computation.9 | convolution fusion | flops 6291456 | bytes 6365184 | tf_op jit(solution)/shard_map/brsij,brsj->bri/dot_general | solution.py:29
  211.3 0.9 fusion.10
  212.3 0.7 bitcast_select_fusion
  (15 shorter events, 0.1 us)
Async XLA Ops:
  0.0 111.3 %copy-start = (bf16[8,6,128,128]{3,2,1,0:T(8,128)(2,1)S(1)}, bf16[8,6,128,128]{3,2,1,0:T(8,128)(2,1)}, u32[]{:S(2)}) copy-start(bf16[8,6,128,128]{3,2,1,0:T(8,128)(2,1)} %param.13) | copy-start | bytes 4718596
  20.2 83.7 %collective-permute-start = (bf16[8,12288]{1,0:T(8,128)(2,1)S(1)}, bf16[8,12288]{1,0:T(8,128)(2,1)S(1)}, u32[]{:S(2)}, u32[]{:S(2)}) collective-permute-start(bf16[8,12288]{1,0:T(8,128)(2,1)S(1)} %all_gather.12), channel_id=1, source_target_pairs={{0,16},{16,32},{32,48},{48,64},{64,80},{80,96},{96,112},{112,128},... | collective-permute-start | bytes 589832 | tf_op jit(solution)/shard_map/ppermute | solution.py:14
  24.0 79.9 %collective-permute-start.1 = (bf16[8,12288]{1,0:T(8,128)(2,1)S(1)}, bf16[8,12288]{1,0:T(8,128)(2,1)S(1)}, u32[]{:S(2)}, u32[]{:S(2)}) collective-permute-start(bf16[8,12288]{1,0:T(8,128)(2,1)S(1)} %all_gather.12), channel_id=1, source_target_pairs={{16,0},{32,16},{48,32},{64,48},{80,64},{96,80},{112,96},{128,112},... | collective-permute-start | bytes 589832 | tf_op jit(solution)/shard_map/ppermute | solution.py:15
  106.7 4.5 %copy-start.3 = (f32[8,768]{1,0:T(8,128)S(1)}, f32[8,768]{1,0:T(8,128)}, u32[]{:S(2)}) copy-start(f32[8,768]{1,0:T(8,128)} %param.12) | copy-start | bytes 73732
  111.3 1.0 copy-start.2
  111.3 27.0 %copy-start.4 = (bf16[8,16,768]{2,1,0:T(8,128)(2,1)S(1)}, bf16[8,16,768]{2,1,0:T(8,128)(2,1)}, u32[]{:S(2)}) copy-start(bf16[8,16,768]{2,1,0:T(8,128)(2,1)} %param.19) | copy-start | bytes 589828
  111.3 92.5 %copy-start.1 = (bf16[8,16,768]{2,1,0:T(8,128)(2,1)S(1)}, bf16[8,16,768]{2,1,0:T(8,128)(2,1)}, u32[]{:S(2)}) copy-start(bf16[8,16,768]{2,1,0:T(8,128)(2,1)} %param.20) | copy-start | bytes 589828
  128.8 75.2 %collective-permute-start.2 = (bf16[8,12288]{1,0:T(8,128)(2,1)S(1)}, bf16[8,12288]{1,0:T(8,128)(2,1)S(1)}, u32[]{:S(2)}, u32[]{:S(2)}) collective-permute-start(bf16[8,12288]{1,0:T(8,128)(2,1)S(1)} %all_gather.14), channel_id=1, source_target_pairs={{0,16},{16,32},{32,48},{48,64},{64,80},{80,96},{96,112},{112,128},... | collective-permute-start | bytes 589832 | tf_op jit(solution)/shard_map/ppermute | solution.py:14
  130.8 73.2 %collective-permute-start.3 = (bf16[8,12288]{1,0:T(8,128)(2,1)S(1)}, bf16[8,12288]{1,0:T(8,128)(2,1)S(1)}, u32[]{:S(2)}, u32[]{:S(2)}) collective-permute-start(bf16[8,12288]{1,0:T(8,128)(2,1)S(1)} %all_gather.14), channel_id=1, source_target_pairs={{16,0},{32,16},{48,32},{64,48},{80,64},{96,80},{112,96},{128,112},... | collective-permute-start | bytes 589832 | tf_op jit(solution)/shard_map/ppermute | solution.py:15
where the time goes:
time: 214 us; the launch traced here: 213 us
  blocking collectives  166 us (78%)
  starting transfers between devices  19.5 us (9%)
  matrix products  13.6 us (6%)
  local copies, waits for them, and re-layouts  7.75 us (4%)
  other arithmetic  5.75 us (3%)
    all_gather x2, blocking collectives, per_device(): all_moments = lax.all_gather(own_moments, 'bubble', axis=0, tiled=True)  74.5 us
    psum x2, blocking collectives, per_device(): own_moments = lax.psum(partial_value, 'panel')  55.7 us
    all_gather x2, blocking collectives, per_device(): panel_full = lax.all_gather(dens_bf, 'panel', axis=1, tiled=True)  35.9 us
    ppermute x2, starting transfers between devices, with_halo(): after = lax.ppermute(first, axis, down)  13.7 us
    dot_general x2, matrix products, near_field(): jnp.einsum('brsij,brsj->bri', near_vals, sources, preferred_element_type=...  9.02 us
    ppermute x2, starting transfers between devices, with_halo(): before = lax.ppermute(last, axis, up)  5.78 us
    gather x2, local copies, waits for them, and re-layouts, near_field(): sources = blocks[local_bubble, near_block]  5.03 us
  transfers between devices with their start and end apart: 4, of which 0 were waited for; matrix products, arithmetic and copies ran while one was open for 4% of the time, Pallas kernels for 0%

commit v1 on v0

--- a/solution.py
+++ b/solution.py
@@ -71,7 +71,8 @@
         partial_value = jnp.einsum(
             "bki,bi->bk", moment_map, dens_bf, preferred_element_type=jnp.float32
         )
-        own_moments = lax.psum(partial_value, "panel")
+        parts = lax.all_gather(partial_value, "panel")
+        own_moments = jnp.sum(parts, axis=0)
         all_moments = lax.all_gather(own_moments, "bubble", axis=0, tiled=True)
         far_coeff = jnp.dot(kernel, all_moments, precision=lax.Precision.HIGHEST).astype(
             jnp.bfloat16

time: 214 us -> 193 us (0.902)
  blocking collectives: 166 us -> 144 us
    psum x2 -> x0, blocking collectives: 55.7 us -> none  [per_device(): own_moments = lax.psum(partial_value, 'panel')]
    all_gather x0 -> x2, blocking collectives: none -> 32.3 us  [per_device(): parts = lax.all_gather(partial_value, 'panel')]
  transfers between devices with their start and end apart: 4 -> 4, of which waited for: 0 -> 0; matrix products, arithmetic and copies ran while one was open for 4% -> 5% of each run, Pallas kernels for 0% -> 0%
where the time goes in v1:
time: 193 us; the launch traced here: 191 us
  blocking collectives  144 us (75%)
  starting transfers between devices  19.5 us (10%)
  matrix products  13.6 us (7%)
  local copies, waits for them, and re-layouts  7.75 us (4%)
  other arithmetic  5.8 us (3%)
    all_gather x2, blocking collectives, per_device(): all_moments = lax.all_gather(own_moments, 'bubble', axis=0, tiled=True)  74.3 us
    all_gather x2, blocking collectives, per_device(): panel_full = lax.all_gather(dens_bf, 'panel', axis=1, tiled=True)  37.8 us
    all_gather x2, blocking collectives, per_device(): parts = lax.all_gather(partial_value, 'panel')  32.3 us
    ppermute x2, starting transfers between devices, with_halo(): after = lax.ppermute(first, axis, down)  13.8 us
    dot_general x2, matrix products, near_field(): jnp.einsum('brsij,brsj->bri', near_vals, sources, preferred_element_type=...  9.02 us
    ppermute x2, starting transfers between devices, with_halo(): before = lax.ppermute(last, axis, up)  5.73 us
    gather x2, local copies, waits for them, and re-layouts, near_field(): sources = blocks[local_bubble, near_block]  5.03 us
  transfers between devices with their start and end apart: 4, of which 0 were waited for; matrix products, arithmetic and copies ran while one was open for 5% of the time, Pallas kernels for 0%

profile of v1, /device:TPU:24, one launch (start us, length us, event | category | flops | bytes accessed | tf_op | source)
XLA Modules:
  0.0 191.3 jit_solution(16642784593482714770)
XLA Ops:
  0.0 0.9 convert_element_type.18
  0.9 19.4 %all_gather.24 = bf16[8,12288]{1,0:T(8,128)(2,1)S(1)} all-gather(bf16[8,768]{1,0:T(8,128)(2,1)S(1)} %convert_element_type.18), channel_id=1, replica_groups=mesh['bubble'=16,'panel'=16] {'panel'}, dimensions={1}, use_global_device_ids=true | all-gather | bytes 208896 | tf_op jit(solution)/shard_map/all_gather | solution.py:66
  20.2 3.8 %collective-permute-start = (bf16[8,12288]{1,0:T(8,128)(2,1)S(1)}, bf16[8,12288]{1,0:T(8,128)(2,1)S(1)}, u32[]{:S(2)}, u32[]{:S(2)}) collective-permute-start(bf16[8,12288]{1,0:T(8,128)(2,1)S(1)} %all_gather.24), channel_id=1, source_target_pairs={{0,16},{16,32},{32,48},{48,64},{64,80},{80,96},{96,112},{112,128},... | collective-permute-start | bytes 589832 | tf_op jit(solution)/shard_map/ppermute | solution.py:14
  24.0 6.2 %collective-permute-start.1 = (bf16[8,12288]{1,0:T(8,128)(2,1)S(1)}, bf16[8,12288]{1,0:T(8,128)(2,1)S(1)}, u32[]{:S(2)}, u32[]{:S(2)}) collective-permute-start(bf16[8,12288]{1,0:T(8,128)(2,1)S(1)} %all_gather.24), channel_id=1, source_target_pairs={{16,0},{32,16},{48,32},{64,48},{80,64},{96,80},{112,96},{128,112},... | collective-permute-start | bytes 589832 | tf_op jit(solution)/shard_map/ppermute | solution.py:15
  30.3 0.8 copy.18
  31.1 0.6 gather_fusion.1
  31.7 0.1 copy.19
  31.8 0.2 slice_reduce_fusion
  31.9 0.7 slice_bitcast_fusion
  32.6 0.7 convert_bitcast_fusion
  33.4 0.8 multiply_reduce_fusion
  34.1 1.1 fusion.16
  35.2 16.2 %all-gather = f32[128,16]{1,0:T(8,128)S(1)} all-gather(f32[8,16]{1,0:T(8,128)S(1)} %bitcast.111), channel_id=2, replica_groups=mesh['bubble'=16,'panel'=16] {'panel'}, dimensions={0}, use_global_device_ids=true | all-gather | bytes 8704 | tf_op jit(solution)/shard_map/all_gather | solution.py:74
  51.4 37.8 %all_gather.27 = f32[128,16]{1,0:T(8,128)S(1)} all-gather(f32[8,16]{1,0:T(8,128)S(1)} %bitcast_reduce_fusion.1), channel_id=1, replica_groups=mesh['bubble'=16,'panel'=16] {'bubble'}, dimensions={0}, use_global_device_ids=true | all-gather | bytes 8704 | tf_op jit(solution)/shard_map/all_gather | solution.py:76
  89.2 0.7 fusion.22
  90.0 0.1 copy.17
  90.1 0.1 reshape.62
  90.2 0.8 iota_compare_fusion
  91.0 0.1 fusion.31
  91.0 0.2 fusion
  91.2 1.1 fusion.34
  92.3 0.7 broadcast_compare_fusion.1
  93.0 0.0 collective-permute-done
  93.0 0.0 collective-permute-done.1
  93.0 0.1 copy.36
  93.1 2.5 %gather_fusion = bf16[192,128]{1,0:T(8,128)(2,1)S(1)} fusion(bf16[24,96,128]{2,1,0:T(8,128)(2,1)S(1)} %bitcast.105, s32[192]{0:T(256)S(1)} %reshape.62), kind=kCustom, calls=%fused_computation | custom fusion | bytes 99840 | tf_op jit(solution)/shard_map/gather | solution.py:26
  95.6 0.1 select_bitcast_fusion.1
  95.7 0.0 copy-start.3
  95.8 4.5 %fusion.4 = f32[8,6,1,128,1]{3,2,4,1,0:T(1,128)S(1)} fusion(bf16[8,6,4,128,128]{4,3,2,1,0:T(8,128)(2,1)} %param.14, bf16[8,6,4,128,1]{3,2,1,0,4:T(4,128)(2,1)S(1)} %select_bitcast_fusion.1), kind=kOutput, calls=%fused_computation.11 | convolution fusion | flops 6291456 | bytes 6365184 | tf_op jit(solution)/shard_map/brsij,brsj->bri/dot_general | solution.py:29
  100.3 0.0 copy-start.1
  100.3 0.9 fusion.14
  101.2 0.1 fusion.36
  101.3 18.4 %all_gather.28 = bf16[8,12288]{1,0:T(8,128)(2,1)S(1)} all-gather(bf16[8,768]{1,0:T(8,128)(2,1)S(1)} %fusion.36), channel_id=1, replica_groups=mesh['bubble'=16,'panel'=16] {'panel'}, dimensions={1}, use_global_device_ids=true | all-gather | bytes 208896 | tf_op jit(solution)/shard_map/all_gather | solution.py:66
  119.8 1.9 collective-permute-start.2
  121.7 7.5 %collective-permute-start.3 = (bf16[8,12288]{1,0:T(8,128)(2,1)S(1)}, bf16[8,12288]{1,0:T(8,128)(2,1)S(1)}, u32[]{:S(2)}, u32[]{:S(2)}) collective-permute-start(bf16[8,12288]{1,0:T(8,128)(2,1)S(1)} %all_gather.28), channel_id=1, source_target_pairs={{16,0},{32,16},{48,32},{64,48},{80,64},{96,80},{112,96},{128,112},... | collective-permute-start | bytes 589832 | tf_op jit(solution)/shard_map/ppermute | solution.py:15
  129.2 0.2 fusion.12
  129.4 16.1 %all-gather.1 = f32[128,16]{1,0:T(8,128)S(1)} all-gather(f32[8,16]{1,0:T(8,128)S(1)} %bitcast.112), channel_id=3, replica_groups=mesh['bubble'=16,'panel'=16] {'panel'}, dimensions={0}, use_global_device_ids=true | all-gather | bytes 8704 | tf_op jit(solution)/shard_map/all_gather | solution.py:74
  145.5 36.5 %all_gather.31 = f32[128,16]{1,0:T(8,128)S(1)} all-gather(f32[8,16]{1,0:T(8,128)S(1)} %bitcast_reduce_fusion), channel_id=1, replica_groups=mesh['bubble'=16,'panel'=16] {'bubble'}, dimensions={0}, use_global_device_ids=true | all-gather | bytes 8704 | tf_op jit(solution)/shard_map/all_gather | solution.py:76
  182.0 0.2 fusion.1
  182.1 0.2 fusion.32
  182.3 0.0 collective-permute-done.2
  182.3 0.1 maximum_bitcast_fusion.1
  182.4 0.1 copy.37
  182.5 2.5 %gather_fusion.2 = bf16[192,128]{1,0:T(8,128)(2,1)S(1)} fusion(bf16[24,96,128]{2,1,0:T(8,128)(2,1)S(1)} %bitcast.104, s32[192]{0:T(256)S(1)} %reshape.62), kind=kCustom, calls=%fused_computation.2 | custom fusion | bytes 99840 | tf_op jit(solution)/shard_map/gather | solution.py:26
  185.0 0.1 select_bitcast_fusion
  185.1 4.5 %fusion.2 = f32[8,6,1,128,1]{3,2,4,1,0:T(1,128)S(1)} fusion(bf16[8,6,4,128,128]{4,3,2,1,0:T(8,128)(2,1)} %param.14, bf16[8,6,4,128,1]{3,2,1,0,4:T(4,128)(2,1)S(1)} %select_bitcast_fusion), kind=kOutput, calls=%fused_computation.9 | convolution fusion | flops 6291456 | bytes 6365184 | tf_op jit(solution)/shard_map/brsij,brsj->bri/dot_general | solution.py:29
  189.7 0.9 fusion.10
  190.6 0.7 bitcast_select_fusion
  (17 shorter events, 0.1 us)
Async XLA Ops:
  0.0 100.3 %copy-start = (bf16[8,6,128,128]{3,2,1,0:T(8,128)(2,1)S(1)}, bf16[8,6,128,128]{3,2,1,0:T(8,128)(2,1)}, u32[]{:S(2)}) copy-start(bf16[8,6,128,128]{3,2,1,0:T(8,128)(2,1)} %param.13) | copy-start | bytes 4718596
  20.2 72.7 %collective-permute-start = (bf16[8,12288]{1,0:T(8,128)(2,1)S(1)}, bf16[8,12288]{1,0:T(8,128)(2,1)S(1)}, u32[]{:S(2)}, u32[]{:S(2)}) collective-permute-start(bf16[8,12288]{1,0:T(8,128)(2,1)S(1)} %all_gather.24), channel_id=1, source_target_pairs={{0,16},{16,32},{32,48},{48,64},{64,80},{80,96},{96,112},{112,128},... | collective-permute-start | bytes 589832 | tf_op jit(solution)/shard_map/ppermute | solution.py:14
  24.0 68.9 %collective-permute-start.1 = (bf16[8,12288]{1,0:T(8,128)(2,1)S(1)}, bf16[8,12288]{1,0:T(8,128)(2,1)S(1)}, u32[]{:S(2)}, u32[]{:S(2)}) collective-permute-start(bf16[8,12288]{1,0:T(8,128)(2,1)S(1)} %all_gather.24), channel_id=1, source_target_pairs={{16,0},{32,16},{48,32},{64,48},{80,64},{96,80},{112,96},{128,112},... | collective-permute-start | bytes 589832 | tf_op jit(solution)/shard_map/ppermute | solution.py:15
  95.7 4.5 %copy-start.3 = (f32[8,768]{1,0:T(8,128)S(1)}, f32[8,768]{1,0:T(8,128)}, u32[]{:S(2)}) copy-start(f32[8,768]{1,0:T(8,128)} %param.12) | copy-start | bytes 73732
  100.3 1.0 copy-start.2
  100.3 28.9 %copy-start.4 = (bf16[8,16,768]{2,1,0:T(8,128)(2,1)S(1)}, bf16[8,16,768]{2,1,0:T(8,128)(2,1)}, u32[]{:S(2)}) copy-start(bf16[8,16,768]{2,1,0:T(8,128)(2,1)} %param.19) | copy-start | bytes 589828
  100.3 81.9 %copy-start.1 = (bf16[8,16,768]{2,1,0:T(8,128)(2,1)S(1)}, bf16[8,16,768]{2,1,0:T(8,128)(2,1)}, u32[]{:S(2)}) copy-start(bf16[8,16,768]{2,1,0:T(8,128)(2,1)} %param.20) | copy-start | bytes 589828
  119.8 62.6 %collective-permute-start.2 = (bf16[8,12288]{1,0:T(8,128)(2,1)S(1)}, bf16[8,12288]{1,0:T(8,128)(2,1)S(1)}, u32[]{:S(2)}, u32[]{:S(2)}) collective-permute-start(bf16[8,12288]{1,0:T(8,128)(2,1)S(1)} %all_gather.28), channel_id=1, source_target_pairs={{0,16},{16,32},{32,48},{48,64},{64,80},{80,96},{96,112},{112,128},... | collective-permute-start | bytes 589832 | tf_op jit(solution)/shard_map/ppermute | solution.py:14
  121.7 60.7 %collective-permute-start.3 = (bf16[8,12288]{1,0:T(8,128)(2,1)S(1)}, bf16[8,12288]{1,0:T(8,128)(2,1)S(1)}, u32[]{:S(2)}, u32[]{:S(2)}) collective-permute-start(bf16[8,12288]{1,0:T(8,128)(2,1)S(1)} %all_gather.28), channel_id=1, source_target_pairs={{16,0},{32,16},{48,32},{64,48},{80,64},{96,80},{112,96},{128,112},... | collective-permute-start | bytes 589832 | tf_op jit(solution)/shard_map/ppermute | solution.py:15
